TPU v7x, 256 devices: a whole 4x4x8 slice. The times are simulated.
256 devices in a mesh: band: 16 (over y, x), lev: 16 (over z, core).
Axes of the slice: x: 4, y: 4, z: 8, core: 2. Of those that a mesh axis runs over, the one named last changes fastest.
Arguments:
- adj_spec: bfloat16 [64, 1280, 2, 1280], P('lev', 'band'), may hold values from -6 to 6
- wave_of_slot: int32 [1280], replicated, may hold values from 0 to 1279, each once
- legendre: bfloat16 [1280, 32, 1280], P('band'), may hold values from -0.15625 to 0.15625
- lat_weight: float32 [32], replicated, may hold values from 0.5 to 1.5
- traj: bfloat16 [64, 64, 5136], P('lev', 'band'), may hold values from -3 to 3
- traj_exp: int32 [64, 64, 4], P('lev', 'band'), may hold values from -2 to 2
- traj_order: int32 [16, 4], P('lev'), may hold values from 0 to 3, each once within a row
- lev_coef: float32 [64], P('lev'), may hold values from 0.02 to 0.2
Outputs:
- adj_out: bfloat16 [64, 1280, 2, 1280], P('lev', 'band')
Inputs may be any that keep to these rules, and one draw needn't show every extreme that they name: `wave_of_slot`: every wavenumber 0 to 1279 is held by exactly one slot. `traj_order`: each row is a permutation of 0 to 3.
All inputs are finite; a program needn't handle non-finite values.
Results may differ from a plain program's by a relative error of at most 0.0085.
Values may be sent and summed in bfloat16 or wider, within the bound.
No kernel may reach another device: no remote copies, remote signals or barrier semaphores. Data moves between devices by JAX's collectives and lax.ppermute only.
A program may use at most 128 MiB of HBM per device.

v0:
```python
import math
import jax
import jax.numpy as jnp
from jax import lax
from jax.sharding import Mesh
from jax.sharding import PartitionSpec as P

NBLK = 4
BAND = ("band_0", "band_1")


def prefix(value, axis, combine, identity):
    size, index = (lax.axis_size(axis), lax.axis_index(axis))
    everything = lax.all_gather(value.astype(jnp.bfloat16), axis)
    start = jnp.broadcast_to(jnp.asarray(identity, value.dtype), value.shape)

    def turn(k, before):
        reached = k < index
        new = combine(before, everything[k].astype(value.dtype))
        return jnp.where(reached, new, before)

    return lax.fori_loop(0, size, turn, start)


def cut_along(value, dim, size):
    lengths = value.shape
    tiles = value.reshape(*lengths[:dim], size, lengths[dim] // size, *lengths[dim + 1 :])
    return jnp.moveaxis(tiles, dim, 0)


def laid_out(tiles, dim):
    tiles = jnp.moveaxis(tiles, 0, dim)
    lengths = tiles.shape
    return tiles.reshape(*lengths[:dim], lengths[dim] * lengths[dim + 1], *lengths[dim + 2 :])


def turned_blocks(tiles, axes, turns):
    inside = tiles.shape[1:]
    whole = tiles.reshape(*(lax.axis_size(a) for a in axes), *inside)
    for k in turns:
        whole = lax.all_to_all(whole, axes[k], k, k, tiled=True)
    return whole.reshape(-1, *inside)


def one_axis_at_a_time(value, axes, turns, split_dim, concat_dim):
    tiles = cut_along(value, split_dim, lax.axis_size(axes))
    return laid_out(turned_blocks(tiles, axes, turns), concat_dim)


def trig_whole(wave_ids, lon_count):
    lon_ids = jnp.arange(lon_count, dtype=jnp.int32)
    phase_int = wave_ids[:, None] * lon_ids[None, :] % lon_count
    angle_rad = phase_int.astype(jnp.float32) * (2.0 * math.pi / lon_count)
    return jnp.stack([jnp.cos(angle_rad), -jnp.sin(angle_rad)], axis=1).astype(jnp.bfloat16)


def add_carry(earlier, later):
    return earlier + later


def body(adj_spec, wave_of_slot, legendre, lat_weight, traj, traj_exp, traj_order, lev_coef):
    highest = lax.Precision.HIGHEST
    levels = adj_spec.shape[0]
    slots = adj_spec.shape[1]
    degrees = adj_spec.shape[3]
    lat_rows = traj.shape[1]
    lon_count = traj.shape[2]
    block_width = lon_count // NBLK
    norm_scale = 1.0 / math.sqrt(degrees)
    first_slot = lax.axis_index(BAND) * slots
    waves_here = lax.dynamic_slice_in_dim(wave_of_slot, first_slot, slots)
    degree_ids = jnp.arange(degrees, dtype=jnp.int32)
    valid_mask = degree_ids[None, :] < (degrees - waves_here)[:, None]
    masked = jnp.where(valid_mask[None, :, None, :], adj_spec, jnp.zeros_like(adj_spec))
    weight_q = jnp.repeat(lat_weight, 2)
    parity_sign = jnp.where(degree_ids % 2 == 0, 1.0, -1.0).astype(jnp.bfloat16)
    stacked = jnp.stack([masked, masked * parity_sign], axis=3)
    side_values = jnp.einsum(
        "lscej,shj->lsche", stacked, legendre, preferred_element_type=jnp.float32
    )
    fourier = (side_values.reshape(levels, slots, 2, -1) * weight_q).astype(jnp.bfloat16)
    fourier_here = lax.all_to_all(fourier, BAND, split_axis=3, concat_axis=1, tiled=True)
    trig_all = trig_whole(wave_of_slot, lon_count)
    order_ids = jnp.arange(levels, dtype=jnp.int32)
    select = (traj_order[0][None, :] == order_ids[:, None]).astype(jnp.float32)
    level_coef = lev_coef[:, None, None]
    grid_list = []
    for block_id in range(NBLK):
        trig_table = trig_all[:, :, block_id * block_width : (block_id + 1) * block_width]
        grid_list.append(
            jnp.einsum(
                "lsca,scw->law", fourier_here, trig_table, preferred_element_type=jnp.float32
            )
            * norm_scale
        )
    grid_all = jnp.stack(grid_list, axis=1)
    running = jnp.cumsum(grid_all, axis=0)
    prior_sum = jnp.concatenate([jnp.zeros_like(grid_all[:1]), running[:-1]], axis=0)
    block_total = running[-1]
    group_carry = prefix(block_total, "lev", add_carry, jnp.zeros_like(block_total))
    above_all = prior_sum + group_carry[None]
    analysis = jnp.zeros((levels, degrees, 2, lat_rows), jnp.float32)
    for block_id in range(NBLK):
        lon_start = block_id * block_width
        trig_table = trig_all[:, :, lon_start : lon_start + block_width]
        exponent = jnp.exp2(traj_exp[:, :, block_id].astype(jnp.float32))
        traj_piece = (
            traj[:, :, lon_start : lon_start + block_width].astype(jnp.float32)
            * exponent[:, :, None]
        )
        traj_value = jnp.einsum("ir,raw->iaw", select, traj_piece, precision=highest)
        forcing = (
            (1.0 + jnp.tanh(traj_value))
            * (grid_all[:, block_id] + level_coef * above_all[:, block_id])
        ).astype(jnp.bfloat16)
        analysis = (
            analysis
            + jnp.einsum("law,scw->lsca", forcing, trig_table, preferred_element_type=jnp.float32)
            * norm_scale
        )
    returned = one_axis_at_a_time(analysis, BAND, (0, 1), 1, 3)
    halves = returned.reshape(levels, slots, 2, -1, 2)
    sym_part = (halves[..., 0] + halves[..., 1]).astype(jnp.bfloat16)
    anti_part = (halves[..., 0] - halves[..., 1]).astype(jnp.bfloat16)
    from_sym = jnp.einsum("lsch,shj->lscj", sym_part, legendre, preferred_element_type=jnp.float32)
    from_anti = jnp.einsum(
        "lsch,shj->lscj", anti_part, legendre, preferred_element_type=jnp.float32
    )
    result = jnp.where(degree_ids % 2 == 0, from_sym, from_anti)
    return jnp.where(valid_mask[None, :, None, :], result, 0.0).astype(jnp.bfloat16)


def solution(mesh):
    torus = Mesh(mesh.devices.reshape(4, 4, mesh.shape["lev"]), ("band_0", "band_1", "lev"))
    return jax.shard_map(
        body,
        mesh=torus,
        in_specs=(
            P("lev", BAND, None, None),
            P(),
            P(BAND, None, None),
            P(),
            P("lev", BAND, None),
            P("lev", BAND, None),
            P("lev", None),
            P("lev"),
        ),
        out_specs=P("lev", BAND, None, None),
        check_vma=False,
    )
```

profile of v0, /device:TPU:2, one launch (start us, length us, event | category | flops | bytes accessed | tf_op | source)
XLA Modules:
  0.0 222.6 jit_solution(7207689764464458243)
XLA Ops:
  0.0 0.8 dynamic-slice_subtract_fusion
  0.8 0.1 iota_compare_fusion
  0.9 3.5 %fusion.94 = (bf16[4,80,2,1,1280]{4,0,3,2,1:T(4,128)(2,1)S(1)}, bf16[4,80,2,1,1280]{4,0,3,2,1:T(4,128)(2,1)S(1)}) fusion(bf16[4,80,2,1280]{3,2,1,0:T(2,128)(2,1)} %param.10, pred[80,1280]{1,0:T(8,128)(4,1)S(1)} %iota_compare_fusion, bf16[1280]{0:T(1024)(128)(2,1)S(1)} %select_convert_fusion.1), kind=kLoop, calls=%fused_computation.79 | loop fusion | flops 1638400 | bytes 5020160 | tf_op jit(solution)/shard_map/stack | solution.py:77
  4.5 6.2 %fusion.89 = f32[4,80,2,32,2]{3,0,4,2,1:T(4,128)S(1)} fusion(bf16[80,32,1280]{2,1,0:T(8,128)(2,1)} %param.12, bf16[4,80,2,1,1280]{4,0,3,2,1:T(4,128)(2,1)S(1)} %get-tuple-element.129, bf16[4,80,2,1,1280]{4,0,3,2,1:T(4,128)(2,1)S(1)} %get-tuple-element.128), kind=kOutput, calls=%fused_computation.78 | convolution fusion | flops 111411200 | bytes 9994240 | tf_op jit(solution)/shard_map/lscej,shj->lsche/dot_general | solution.py:78
  10.6 0.3 copy.69
  11.0 0.1 mul.183
  11.1 0.1 multiply_convert_fusion
  11.2 0.8 copy.70
  12.0 7.5 %all-to-all-start = ((bf16[4,80,2,64]{1,2,0,3:T(2,128)(2,1)}), bf16[4,80,2,64]{1,2,0,3:T(2,128)(2,1)S(1)}, u32[]{:S(2)}, u32[]{:S(2)}) async-start(bf16[4,80,2,64]{1,2,0,3:T(2,128)(2,1)} %copy.70), calls=%async_computation | async-start | bytes 262144 | tf_op jit(solution)/shard_map/all_to_all | solution.py:82
  19.5 109.3 %cosine_convert_fusion = (bf16[1280,1,5136]{0,2,1:T(8,128)(2,1)S(1)}, bf16[1280,1,5136]{0,2,1:T(8,128)(2,1)S(1)}) fusion(s32[1280]{0:T(1024)S(1)} %copy-done.3), kind=kLoop, calls=%fused_computation.11 | loop fusion | flops 78888960 | bytes 26301440 | tf_op jit(solution)/shard_map/convert.2
  128.8 0.2 exponential_reduce_fusion.3
  129.0 10.5 %fusion.6 = (bf16[1280,2,1284]{0,2,1:T(8,128)(2,1)}, bf16[1280,2,1284]{0,2,1:T(8,128)(2,1)}, bf16[1280,2,1284]{0,2,1:T(8,128)(2,1)}, bf16[1280,2,1284]{0,2,1:T(8,128)(2,1)}) fusion(bf16[1280,1,5136]{0,2,1:T(8,128)(2,1)S(1)} %get-tuple-element.136, bf16[1280,1,5136]{0,2,1:T(8,128)(2,1)S(1)} %get-tuple-element.137), kind=kLoop, calls=%fused_computation.17 | loop fusion | flops 52592640 | bytes 52592640 | tf_op jit(solution)/shard_map/stack | solution.py:54
  139.5 0.2 convert_multiply_fusion.3
  139.8 0.2 reshape.151
  140.0 5.0 %fusion.74 = f32[4,4,1284]{2,0,1:T(4,128)S(1)} fusion(bf16[4,1280,2,4]{1,0,2,3:T(4,128)(2,1)S(1)} %reshape.151, bf16[1280,2,1284]{0,2,1:T(8,128)(2,1)} %get-tuple-element.126), kind=kOutput, calls=%fused_computation.59 | convolution fusion | flops 105205824 | bytes 6738176 | tf_op jit(solution)/shard_map/lsca,scw->law/dot_general | solution.py:91
  145.0 5.0 %fusion.68 = f32[4,4,1284]{2,0,1:T(4,128)S(1)} fusion(bf16[4,1280,2,4]{1,0,2,3:T(4,128)(2,1)S(1)} %reshape.151, bf16[1280,2,1284]{0,2,1:T(8,128)(2,1)} %get-tuple-element.127), kind=kOutput, calls=%fused_computation.57 | convolution fusion | flops 105205824 | bytes 6738176 | tf_op jit(solution)/shard_map/lsca,scw->law/dot_general | solution.py:91
  150.0 2.0 fusion.62
  152.0 2.0 fusion.56
  154.1 0.5 reduce_window_sum.11
  154.6 0.1 slice.160
  154.7 22.2 %all_gather.4 = bf16[16,4,4,1284]{3,2,1,0:T(4,128)(2,1)S(1)} all-gather(bf16[1,4,4,1284]{3,2,1,0:T(4,128)(2,1)S(1)} %copy.77), channel_id=1, replica_groups=mesh['band_0'=4,'band_1'=4,'lev'=16] {'lev'}, dimensions={0}, use_global_device_ids=true | all-gather | bytes 698496 | tf_op jit(solution)/shard_map/all_gather | solution.py:14
  176.9 1.7 while.14
  177.4 0.1 add_select_fusion.4
  178.6 0.2 pad_add_fusion
  178.8 0.2 fusion.88
  179.0 4.3 %fusion.8 = f32[1280,2,4,4]{0,3,2,1:T(4,128)S(1)} fusion(bf16[1280,2,1284]{0,2,1:T(8,128)(2,1)} %get-tuple-element.126, bf16[4,4,1284]{2,0,1:T(4,128)(2,1)S(1)} %fusion.88), kind=kOutput, calls=%fused_computation.20 | convolution fusion | flops 105185280 | bytes 6779008 | tf_op jit(solution)/shard_map/law,scw->lsca/dot_general | solution.py:118
  183.3 0.2 fusion.87
  183.6 1.2 fusion.10
  184.8 0.2 fusion.86
  185.1 0.4 slice-done.5
  185.5 1.2 fusion.12
  186.7 0.2 fusion.85
  187.0 0.4 slice-done.3
  187.4 1.2 fusion.50
  188.7 0.2 reshape.131
  188.9 0.1 copy.86
  189.0 11.2 %all_to_all.28 = f32[4,4,4,80,2,4]{3,5,1,4,2,0:T(4,128)S(1)} all-to-all(f32[4,4,4,80,2,4]{3,5,1,4,2,0:T(4,128)S(1)} %copy.86), channel_id=1, replica_groups=mesh['band_0'=4,'band_1'=4,'lev'=16] {'band_0'}, dimensions={0} | all-to-all | bytes 327680 | tf_op jit(solution)/shard_map/all_to_all | solution.py:41
  200.3 0.8 copy.87
  201.0 4.8 %all-to-all-start.2 = ((f32[4,4,4,80,2,4]{3,5,0,4,2,1:T(4,128)}), f32[4,4,4,80,2,4]{3,5,0,4,2,1:T(4,128)S(1)}, u32[]{:S(2)}, u32[]{:S(2)}) async-start(f32[4,4,4,80,2,4]{3,5,0,4,2,1:T(4,128)} %copy.87), calls=%async_computation.2 | async-start | bytes 524288 | tf_op jit(solution)/shard_map/all_to_all | solution.py:41
  205.8 5.2 %all-to-all-done.2 = f32[4,4,4,80,2,4]{3,5,0,4,2,1:T(4,128)S(1)} async-done(((f32[4,4,4,80,2,4]{3,5,0,4,2,1:T(4,128)}), f32[4,4,4,80,2,4]{3,5,0,4,2,1:T(4,128)S(1)}, u32[]{:S(2)}, u32[]{:S(2)}) %all-to-all-start.2) | async-done | bytes 163872 | tf_op jit(solution)/shard_map/all_to_all | solution.py:41
  211.0 0.2 copy.88
  211.2 0.1 copy.89
  211.3 0.3 add_convert_fusion
  211.6 0.2 copy.111
  211.8 3.8 %fusion.26 = bf16[80,4,2,1280]{3,1,2,0:T(4,128)(2,1)S(1)} fusion(bf16[80,32,1280]{2,1,0:T(8,128)(2,1)} %param.12, bf16[4,80,2,32,1]{3,0,2,1,4:T(4,128)(2,1)S(1)} %copy.111), kind=kOutput, calls=%fused_computation.38 | convolution fusion | flops 52428800 | bytes 8232960 | tf_op jit(solution)/shard_map/lsch,shj->lscj/dot_general | solution.py:126
  215.6 0.2 copy.110
  215.8 4.4 %fusion.35 = bf16[4,80,2,1280]{3,0,2,1:T(4,128)(2,1)S(1)} fusion(bf16[80,4,2,1280]{3,1,2,0:T(4,128)(2,1)S(1)} %fusion.26, bf16[80,32,1280]{2,1,0:T(8,128)(2,1)} %param.12, pred[1280]{0:T(1024)(128)(4,1)S(1)} %fusion.117, pred[80,1280]{1,0:T(8,128)(4,1)S(1)} %iota_compare_fusion, bf16[4,80,2,32,1]{3,0,2,1,4:T(4,128)(2,1)S(1)} %copy.110), kind=kOutput, calls=%fused_computation.46 | convolution fusion | flops 54067200 | bytes 9975040 | tf_op jit(solution)/shard_map/lsch,shj->lscj/dot_general | solution.py:125
  220.2 2.4 %copy.92 = bf16[4,80,2,1280]{3,2,1,0:T(2,128)(2,1)} copy(bf16[4,80,2,1280]{3,0,2,1:T(4,128)(2,1)S(1)} %fusion.35) | data formatting | bytes 3276800 | tf_op jit(solution)/shard_map/convert_element_type | solution.py:130
  (57 shorter events, 1.7 us)
Async XLA Ops:
  4.5 6.5 %copy-start.4 = (f32[32]{0:T(128)S(1)}, f32[32]{0:T(128)}, u32[]{:S(2)}) copy-start(f32[32]{0:T(128)} %param.13) | copy-start | bytes 388
  4.5 15.0 %copy-start.3 = (s32[1280]{0:T(1024)S(1)}, s32[1280]{0:T(1024)}, u32[]{:S(2)}) copy-start(s32[1280]{0:T(1024)} %param.11) | copy-start | bytes 15364
  12.0 127.7 %all-to-all-start = ((bf16[4,80,2,64]{1,2,0,3:T(2,128)(2,1)}), bf16[4,80,2,64]{1,2,0,3:T(2,128)(2,1)S(1)}, u32[]{:S(2)}, u32[]{:S(2)}) async-start(bf16[4,80,2,64]{1,2,0,3:T(2,128)(2,1)} %copy.70), calls=%async_computation | async-start | bytes 262144 | tf_op jit(solution)/shard_map/all_to_all | solution.py:82
  19.5 109.3 %copy-start.2 = (s32[4,4,4]{2,1,0:T(4,128)S(1)}, s32[4,4,4]{2,1,0:T(4,128)}, u32[]{:S(2)}) copy-start(s32[4,4,4]{2,1,0:T(4,128)} %param.15) | copy-start | bytes 772
  129.0 10.5 %copy-start.1 = (bf16[4,4,5136]{2,1,0:T(4,128)(2,1)S(1)}, bf16[4,4,5136]{2,1,0:T(4,128)(2,1)}, u32[]{:S(2)}) copy-start(bf16[4,4,5136]{2,1,0:T(4,128)(2,1)} %param.14) | copy-start | bytes 493060
  140.0 10.0 %copy-start = (bf16[1280,2,1284]{0,2,1:T(8,128)(2,1)S(1)}, bf16[1280,2,1284]{0,2,1:T(8,128)(2,1)}, u32[]{:S(2)}) copy-start(bf16[1280,2,1284]{0,2,1:T(8,128)(2,1)} %get-tuple-element.125) | copy-start | bytes 19722244
  140.0 12.0 %slice-start = ((s8[6594560]{0:T(1024)(128)(4,1)}), s8[4194304]{0:T(1024)(128)(4,1)S(1)}, s32[]{:S(2)}) async-start(s8[6594560]{0:T(1024)(128)(4,1)} %bitcast.188), calls=%async_computation.3 | async-start | bytes 8388608
  145.0 7.0 %slice-start.1 = ((s8[6594560]{0:T(1024)(128)(4,1)}), s8[2400256]{0:T(1024)(128)(4,1)S(1)}, s32[]{:S(2)}) async-start(s8[6594560]{0:T(1024)(128)(4,1)} %bitcast.188), calls=%async_computation.4 | async-start | bytes 4800512
  151.9 26.8 %copy-start.5 = (f32[4]{0:T(128)S(1)}, f32[4]{0:T(128)}, u32[]{:S(2)}) copy-start(f32[4]{0:T(128)} %param.17) | copy-start | bytes 52
  151.9 26.8 %copy-start.6 = (s32[1,4]{1,0:T(1,128)S(1)}, s32[1,4]{1,0:T(1,128)}, u32[]{:S(2)}) copy-start(s32[1,4]{1,0:T(1,128)} %param.16) | copy-start | bytes 52
  178.6 5.0 %slice-start.6 = ((s8[6594560]{0:T(1024)(128)(4,1)}), s8[4194304]{0:T(1024)(128)(4,1)S(1)}, s32[]{:S(2)}) async-start(s8[6594560]{0:T(1024)(128)(4,1)} %bitcast.194), calls=%async_computation.9 | async-start | bytes 8388608
  179.0 4.6 %slice-start.7 = ((s8[6594560]{0:T(1024)(128)(4,1)}), s8[2400256]{0:T(1024)(128)(4,1)S(1)}, s32[]{:S(2)}) async-start(s8[6594560]{0:T(1024)(128)(4,1)} %bitcast.194), calls=%async_computation.10 | async-start | bytes 4800512
  179.0 6.1 %slice-start.4 = ((s8[6594560]{0:T(1024)(128)(4,1)}), s8[4194304]{0:T(1024)(128)(4,1)S(1)}, s32[]{:S(2)}) async-start(s8[6594560]{0:T(1024)(128)(4,1)} %bitcast.192), calls=%async_computation.7 | async-start | bytes 8388608
  183.6 1.9 slice-start.5
  183.6 3.4 %slice-start.2 = ((s8[6594560]{0:T(1024)(128)(4,1)}), s8[4194304]{0:T(1024)(128)(4,1)S(1)}, s32[]{:S(2)}) async-start(s8[6594560]{0:T(1024)(128)(4,1)} %bitcast.190), calls=%async_computation.5 | async-start | bytes 8388608
  185.5 1.9 slice-start.3
  201.0 10.0 %all-to-all-start.2 = ((f32[4,4,4,80,2,4]{3,5,0,4,2,1:T(4,128)}), f32[4,4,4,80,2,4]{3,5,0,4,2,1:T(4,128)S(1)}, u32[]{:S(2)}, u32[]{:S(2)}) async-start(f32[4,4,4,80,2,4]{3,5,0,4,2,1:T(4,128)} %copy.87), calls=%async_computation.2 | async-start | bytes 524288 | tf_op jit(solution)/shard_map/all_to_all | solution.py:41
where the time goes:
time: 223 us
  other arithmetic  127 us (57%)
  matrix products  37.2 us (17%)
  blocking collectives  33.4 us (15%)
  starting transfers between devices  12.3 us (6%)
  local copies, waits for them, and re-layouts  6.71 us (3%)
  waiting for transfers between devices  5.22 us (2%)
    another operation x1, other arithmetic  109 us
    all_gather x1, blocking collectives, prefix(): everything = lax.all_gather(value.astype(jnp.bfloat16), axis)  22.2 us
    dot_general x4, matrix products, body(): jnp.einsum('lsca,scw->law', fourier_here, trig_table, preferred_element_t...  13.9 us
    all_to_all x1, blocking collectives, turned_blocks(): whole = lax.all_to_all(whole, axes[k], k, k, tiled=True)  11.2 us
    another operation x1, other arithmetic, trig_whole(): jnp.stack([jnp.cos(angle_rad), -jnp.sin(angle_rad)], axis=1)  10.5 us
    dot_general x4, matrix products, body(): jnp.einsum('law,scw->lsca', forcing, trig_table, preferred_element_type=j...  8 us
    all_to_all x1, starting transfers between devices, body(): lax.all_to_all(fourier, BAND, split_axis=3, concat_axis=1, tiled=True)  7.48 us
    dot_general x1, matrix products, body(): jnp.einsum('lscej,shj->lsche', stacked, legendre, preferred_element_type=...  6.16 us
  transfers between devices with their start and end apart: 2, of which 1 were waited for; matrix products, arithmetic and copies ran while one was open for 54% of the time, Pallas kernels for 0%

commit v1 on v0

--- a/solution.py
+++ b/solution.py
@@ -79,7 +79,10 @@
         "lscej,shj->lsche", stacked, legendre, preferred_element_type=jnp.float32
     )
     fourier = (side_values.reshape(levels, slots, 2, -1) * weight_q).astype(jnp.bfloat16)
-    fourier_here = lax.all_to_all(fourier, BAND, split_axis=3, concat_axis=1, tiled=True)
+    fourier_here = jnp.concatenate(
+        lax.all_to_all(jnp.stack(jnp.split(fourier, lax.axis_size(BAND), axis=3)), BAND, 0, 0),
+        axis=1,
+    )
     trig_all = trig_whole(wave_of_slot, lon_count)
     order_ids = jnp.arange(levels, dtype=jnp.int32)
     select = (traj_order[0][None, :] == order_ids[:, None]).astype(jnp.float32)

time: 223 us -> 232 us (1.040)
  local copies, waits for them, and re-layouts: 6.71 us -> 15.6 us
    unnamed x30 -> x45, local copies, waits for them, and re-layouts: 0.96 us -> 10 us
  transfers between devices with their start and end apart: 2 -> 2, of which waited for: 1 -> 1; matrix products, arithmetic and copies ran while one was open for 54% -> 52% of each run, Pallas kernels for 0% -> 0%
where the time goes in v1:
time: 232 us
  other arithmetic  127 us (55%)
  matrix products  37.2 us (16%)
  blocking collectives  33.4 us (14%)
  local copies, waits for them, and re-layouts  15.6 us (7%)
  starting transfers between devices  12.3 us (5%)
  waiting for transfers between devices  5.22 us (2%)
    another operation x1, other arithmetic  109 us
    all_gather x1, blocking collectives, prefix(): everything = lax.all_gather(value.astype(jnp.bfloat16), axis)  22.2 us
    dot_general x4, matrix products, body(): jnp.einsum('lsca,scw->law', fourier_here, trig_table, preferred_element_t...  13.9 us
    all_to_all x1, blocking collectives, turned_blocks(): whole = lax.all_to_all(whole, axes[k], k, k, tiled=True)  11.2 us
    another operation x1, other arithmetic, trig_whole(): jnp.stack([jnp.cos(angle_rad), -jnp.sin(angle_rad)], axis=1)  10.5 us
    unnamed x45, local copies, waits for them, and re-layouts  10 us
    dot_general x4, matrix products, body(): jnp.einsum('law,scw->lsca', forcing, trig_table, preferred_element_type=j...  8 us
    all_to_all x1, starting transfers between devices, body(): lax.all_to_all(jnp.stack(jnp.split(fourier, lax.axis_size(BAND), axis=3))...  7.48 us
  transfers between devices with their start and end apart: 2, of which 1 were waited for; matrix products, arithmetic and copies ran while one was open for 52% of the time, Pallas kernels for 0%

profile of v1, /device:TPU:2, one launch (start us, length us, event | category | flops | bytes accessed | tf_op | source)
XLA Modules:
  0.0 231.5 jit_solution(15794193014706480578)
XLA Ops:
  0.0 0.8 dynamic-slice_subtract_fusion
  0.9 3.5 %fusion.94 = (bf16[4,80,2,1,1280]{4,0,3,2,1:T(4,128)(2,1)S(1)}, bf16[4,80,2,1,1280]{4,0,3,2,1:T(4,128)(2,1)S(1)}) fusion(bf16[4,80,2,1280]{3,2,1,0:T(2,128)(2,1)} %param.10, pred[80,1280]{1,0:T(8,128)(4,1)S(1)} %iota_compare_fusion, bf16[1280]{0:T(1024)(128)(2,1)S(1)} %select_convert_fusion.1), kind=kLoop, calls=%fused_computation.79 | loop fusion | flops 1638400 | bytes 5020160 | tf_op jit(solution)/shard_map/stack | solution.py:77
  4.5 6.2 %fusion.89 = f32[4,80,2,32,2]{3,0,4,2,1:T(4,128)S(1)} fusion(bf16[80,32,1280]{2,1,0:T(8,128)(2,1)} %param.12, bf16[4,80,2,1,1280]{4,0,3,2,1:T(4,128)(2,1)S(1)} %get-tuple-element.129, bf16[4,80,2,1,1280]{4,0,3,2,1:T(4,128)(2,1)S(1)} %get-tuple-element.128), kind=kOutput, calls=%fused_computation.78 | convolution fusion | flops 111411200 | bytes 9994240 | tf_op jit(solution)/shard_map/lscej,shj->lsche/dot_general | solution.py:78
  10.6 0.3 copy.82
  11.2 0.6 constant_dynamic-update-slice_fusion.15
  11.8 0.6 constant_dynamic-update-slice_fusion.14
  12.4 0.6 constant_dynamic-update-slice_fusion.13
  13.1 0.6 constant_dynamic-update-slice_fusion.12
  13.7 0.6 constant_dynamic-update-slice_fusion.11
  14.3 0.6 constant_dynamic-update-slice_fusion.10
  14.9 0.6 constant_dynamic-update-slice_fusion.9
  15.5 0.6 constant_dynamic-update-slice_fusion.8
  16.1 0.6 constant_dynamic-update-slice_fusion.7
  16.7 0.6 constant_dynamic-update-slice_fusion.6
  17.3 0.6 constant_dynamic-update-slice_fusion.5
  17.9 0.6 constant_dynamic-update-slice_fusion.4
  18.5 0.6 constant_dynamic-update-slice_fusion.3
  19.1 0.6 constant_dynamic-update-slice_fusion.2
  19.7 0.6 constant_dynamic-update-slice_fusion.1
  20.3 0.6 constant_dynamic-update-slice_fusion
  20.9 7.5 %all-to-all-start = ((bf16[16,4,80,2,4]{2,4,3,1,0:T(4,128)(2,1)}), bf16[16,4,80,2,4]{2,4,3,1,0:T(4,128)(2,1)S(1)}, u32[]{:S(2)}, u32[]{:S(2)}) async-start(bf16[16,4,80,2,4]{2,4,3,1,0:T(4,128)(2,1)} %constant_dynamic-update-slice_fusion), calls=%async_computation | async-start | bytes 262144 | tf_op jit(solution)/shard_map/all_to_all | solution.py:83
  28.4 109.3 %cosine_convert_fusion = (bf16[1280,1,5136]{0,2,1:T(8,128)(2,1)S(1)}, bf16[1280,1,5136]{0,2,1:T(8,128)(2,1)S(1)}) fusion(s32[1280]{0:T(1024)S(1)} %copy-done.3), kind=kLoop, calls=%fused_computation.11 | loop fusion | flops 78888960 | bytes 26301440 | tf_op jit(solution)/shard_map/convert.2
  137.9 10.5 %fusion.6 = (bf16[1280,2,1284]{0,2,1:T(8,128)(2,1)}, bf16[1280,2,1284]{0,2,1:T(8,128)(2,1)}, bf16[1280,2,1284]{0,2,1:T(8,128)(2,1)}, bf16[1280,2,1284]{0,2,1:T(8,128)(2,1)}) fusion(bf16[1280,1,5136]{0,2,1:T(8,128)(2,1)S(1)} %get-tuple-element.136, bf16[1280,1,5136]{0,2,1:T(8,128)(2,1)S(1)} %get-tuple-element.137), kind=kLoop, calls=%fused_computation.17 | loop fusion | flops 52592640 | bytes 52592640 | tf_op jit(solution)/shard_map/stack | solution.py:54
  148.9 5.0 %fusion.74 = f32[4,4,1284]{2,0,1:T(4,128)S(1)} fusion(bf16[4,1280,2,4]{1,0,2,3:T(4,128)(2,1)S(1)} %reshape.159, bf16[1280,2,1284]{0,2,1:T(8,128)(2,1)} %get-tuple-element.126), kind=kOutput, calls=%fused_computation.59 | convolution fusion | flops 105205824 | bytes 6738176 | tf_op jit(solution)/shard_map/lsca,scw->law/dot_general | solution.py:94
  153.9 5.0 %fusion.68 = f32[4,4,1284]{2,0,1:T(4,128)S(1)} fusion(bf16[4,1280,2,4]{1,0,2,3:T(4,128)(2,1)S(1)} %reshape.159, bf16[1280,2,1284]{0,2,1:T(8,128)(2,1)} %get-tuple-element.127), kind=kOutput, calls=%fused_computation.57 | convolution fusion | flops 105205824 | bytes 6738176 | tf_op jit(solution)/shard_map/lsca,scw->law/dot_general | solution.py:94
  158.9 2.0 fusion.62
  160.9 2.0 fusion.56
  163.0 0.5 reduce_window_sum.11
  163.6 22.2 %all_gather.4 = bf16[16,4,4,1284]{3,2,1,0:T(4,128)(2,1)S(1)} all-gather(bf16[1,4,4,1284]{3,2,1,0:T(4,128)(2,1)S(1)} %copy.88), channel_id=1, replica_groups=mesh['band_0'=4,'band_1'=4,'lev'=16] {'lev'}, dimensions={0}, use_global_device_ids=true | all-gather | bytes 698496 | tf_op jit(solution)/shard_map/all_gather | solution.py:14
  185.8 1.7 while.14
  187.7 0.2 fusion.88
  187.9 4.3 %fusion.8 = f32[1280,2,4,4]{0,3,2,1:T(4,128)S(1)} fusion(bf16[1280,2,1284]{0,2,1:T(8,128)(2,1)} %get-tuple-element.126, bf16[4,4,1284]{2,0,1:T(4,128)(2,1)S(1)} %fusion.88), kind=kOutput, calls=%fused_computation.20 | convolution fusion | flops 105185280 | bytes 6779008 | tf_op jit(solution)/shard_map/law,scw->lsca/dot_general | solution.py:121
  192.2 0.2 fusion.87
  192.5 1.2 fusion.10
  193.7 0.2 fusion.86
  194.0 0.4 slice-done.5
  194.4 1.2 fusion.12
  195.7 0.2 fusion.85
  195.9 0.4 slice-done.3
  196.4 1.2 fusion.50
  197.9 11.2 %all_to_all.15 = f32[4,4,4,80,2,4]{3,5,1,4,2,0:T(4,128)S(1)} all-to-all(f32[4,4,4,80,2,4]{3,5,1,4,2,0:T(4,128)S(1)} %copy.97), channel_id=1, replica_groups=mesh['band_0'=4,'band_1'=4,'lev'=16] {'band_0'}, dimensions={0} | all-to-all | bytes 327680 | tf_op jit(solution)/shard_map/all_to_all | solution.py:41
  209.2 0.8 copy.98
  209.9 4.8 %all-to-all-start.2 = ((f32[4,4,4,80,2,4]{3,5,0,4,2,1:T(4,128)}), f32[4,4,4,80,2,4]{3,5,0,4,2,1:T(4,128)S(1)}, u32[]{:S(2)}, u32[]{:S(2)}) async-start(f32[4,4,4,80,2,4]{3,5,0,4,2,1:T(4,128)} %copy.98), calls=%async_computation.2 | async-start | bytes 524288 | tf_op jit(solution)/shard_map/all_to_all | solution.py:41
  214.7 5.2 %all-to-all-done.2 = f32[4,4,4,80,2,4]{3,5,0,4,2,1:T(4,128)S(1)} async-done(((f32[4,4,4,80,2,4]{3,5,0,4,2,1:T(4,128)}), f32[4,4,4,80,2,4]{3,5,0,4,2,1:T(4,128)S(1)}, u32[]{:S(2)}, u32[]{:S(2)}) %all-to-all-start.2) | async-done | bytes 163872 | tf_op jit(solution)/shard_map/all_to_all | solution.py:41
  220.2 0.3 add_convert_fusion
  220.7 3.8 %fusion.26 = bf16[80,4,2,1280]{3,1,2,0:T(4,128)(2,1)S(1)} fusion(bf16[80,32,1280]{2,1,0:T(8,128)(2,1)} %param.12, bf16[4,80,2,32,1]{3,0,2,1,4:T(4,128)(2,1)S(1)} %copy.122), kind=kOutput, calls=%fused_computation.38 | convolution fusion | flops 52428800 | bytes 8232960 | tf_op jit(solution)/shard_map/lsch,shj->lscj/dot_general | solution.py:129
  224.7 4.4 %fusion.35 = bf16[4,80,2,1280]{3,0,2,1:T(4,128)(2,1)S(1)} fusion(bf16[80,4,2,1280]{3,1,2,0:T(4,128)(2,1)S(1)} %fusion.26, bf16[80,32,1280]{2,1,0:T(8,128)(2,1)} %param.12, pred[1280]{0:T(1024)(128)(4,1)S(1)} %fusion.117, pred[80,1280]{1,0:T(8,128)(4,1)S(1)} %iota_compare_fusion, bf16[4,80,2,32,1]{3,0,2,1,4:T(4,128)(2,1)S(1)} %copy.121), kind=kOutput, calls=%fused_computation.46 | convolution fusion | flops 54067200 | bytes 9975040 | tf_op jit(solution)/shard_map/lsch,shj->lscj/dot_general | solution.py:128
  229.1 2.4 %copy.103 = bf16[4,80,2,1280]{3,2,1,0:T(2,128)(2,1)} copy(bf16[4,80,2,1280]{3,0,2,1:T(4,128)(2,1)S(1)} %fusion.35) | data formatting | bytes 3276800 | tf_op jit(solution)/shard_map/convert_element_type | solution.py:133
  (71 shorter events, 3.8 us)
Async XLA Ops:
  4.5 6.5 %copy-start.4 = (f32[32]{0:T(128)S(1)}, f32[32]{0:T(128)}, u32[]{:S(2)}) copy-start(f32[32]{0:T(128)} %param.13) | copy-start | bytes 388
  4.5 24.0 %copy-start.3 = (s32[1280]{0:T(1024)S(1)}, s32[1280]{0:T(1024)}, u32[]{:S(2)}) copy-start(s32[1280]{0:T(1024)} %param.11) | copy-start | bytes 15364
  20.9 127.7 %all-to-all-start = ((bf16[16,4,80,2,4]{2,4,3,1,0:T(4,128)(2,1)}), bf16[16,4,80,2,4]{2,4,3,1,0:T(4,128)(2,1)S(1)}, u32[]{:S(2)}, u32[]{:S(2)}) async-start(bf16[16,4,80,2,4]{2,4,3,1,0:T(4,128)(2,1)} %constant_dynamic-update-slice_fusion), calls=%async_computation | async-start | bytes 262144 | tf_op jit(solution)/shard_map/all_to_all | solution.py:83
  28.4 109.3 %copy-start.2 = (s32[4,4,4]{2,1,0:T(4,128)S(1)}, s32[4,4,4]{2,1,0:T(4,128)}, u32[]{:S(2)}) copy-start(s32[4,4,4]{2,1,0:T(4,128)} %param.15) | copy-start | bytes 772
  137.9 10.5 %copy-start.1 = (bf16[4,4,5136]{2,1,0:T(4,128)(2,1)S(1)}, bf16[4,4,5136]{2,1,0:T(4,128)(2,1)}, u32[]{:S(2)}) copy-start(bf16[4,4,5136]{2,1,0:T(4,128)(2,1)} %param.14) | copy-start | bytes 493060
  148.9 10.0 %copy-start = (bf16[1280,2,1284]{0,2,1:T(8,128)(2,1)S(1)}, bf16[1280,2,1284]{0,2,1:T(8,128)(2,1)}, u32[]{:S(2)}) copy-start(bf16[1280,2,1284]{0,2,1:T(8,128)(2,1)} %get-tuple-element.125) | copy-start | bytes 19722244
  148.9 12.0 %slice-start = ((s8[6594560]{0:T(1024)(128)(4,1)}), s8[4194304]{0:T(1024)(128)(4,1)S(1)}, s32[]{:S(2)}) async-start(s8[6594560]{0:T(1024)(128)(4,1)} %bitcast.250), calls=%async_computation.3 | async-start | bytes 8388608
  153.9 7.0 %slice-start.1 = ((s8[6594560]{0:T(1024)(128)(4,1)}), s8[2400256]{0:T(1024)(128)(4,1)S(1)}, s32[]{:S(2)}) async-start(s8[6594560]{0:T(1024)(128)(4,1)} %bitcast.250), calls=%async_computation.4 | async-start | bytes 4800512
  160.8 26.8 %copy-start.5 = (f32[4]{0:T(128)S(1)}, f32[4]{0:T(128)}, u32[]{:S(2)}) copy-start(f32[4]{0:T(128)} %param.17) | copy-start | bytes 52
  160.9 26.8 %copy-start.6 = (s32[1,4]{1,0:T(1,128)S(1)}, s32[1,4]{1,0:T(1,128)}, u32[]{:S(2)}) copy-start(s32[1,4]{1,0:T(1,128)} %param.16) | copy-start | bytes 52
  187.5 5.0 %slice-start.6 = ((s8[6594560]{0:T(1024)(128)(4,1)}), s8[4194304]{0:T(1024)(128)(4,1)S(1)}, s32[]{:S(2)}) async-start(s8[6594560]{0:T(1024)(128)(4,1)} %bitcast.256), calls=%async_computation.9 | async-start | bytes 8388608
  187.9 4.6 %slice-start.7 = ((s8[6594560]{0:T(1024)(128)(4,1)}), s8[2400256]{0:T(1024)(128)(4,1)S(1)}, s32[]{:S(2)}) async-start(s8[6594560]{0:T(1024)(128)(4,1)} %bitcast.256), calls=%async_computation.10 | async-start | bytes 4800512
  187.9 6.1 %slice-start.4 = ((s8[6594560]{0:T(1024)(128)(4,1)}), s8[4194304]{0:T(1024)(128)(4,1)S(1)}, s32[]{:S(2)}) async-start(s8[6594560]{0:T(1024)(128)(4,1)} %bitcast.254), calls=%async_computation.7 | async-start | bytes 8388608
  192.5 1.9 slice-start.5
  192.5 3.4 %slice-start.2 = ((s8[6594560]{0:T(1024)(128)(4,1)}), s8[4194304]{0:T(1024)(128)(4,1)S(1)}, s32[]{:S(2)}) async-start(s8[6594560]{0:T(1024)(128)(4,1)} %bitcast.252), calls=%async_computation.5 | async-start | bytes 8388608
  194.4 1.9 slice-start.3
  209.9 10.0 %all-to-all-start.2 = ((f32[4,4,4,80,2,4]{3,5,0,4,2,1:T(4,128)}), f32[4,4,4,80,2,4]{3,5,0,4,2,1:T(4,128)S(1)}, u32[]{:S(2)}, u32[]{:S(2)}) async-start(f32[4,4,4,80,2,4]{3,5,0,4,2,1:T(4,128)} %copy.98), calls=%async_computation.2 | async-start | bytes 524288 | tf_op jit(solution)/shard_map/all_to_all | solution.py:41
